TPU v7x, 32 devices: a whole 2x2x4 slice. The times are simulated.
32 devices in a mesh: fsdp: 4 (over z), adapter: 8 (over y, x, core).
Axes of the slice: x: 2, y: 2, z: 4, core: 2. Of those that a mesh axis runs over, the one named last changes fastest.
Arguments:
- tokens: bfloat16 [2048, 8192], P('adapter', 'fsdp'), may hold values from -6 to 6
- tenant: int32 [2048], P('adapter'), may hold values from 0 to 63, as said below
- send_list: int32 [8, 8, 128], P('adapter'), may hold values from -1 to 255, as said below
- base_weight: bfloat16 [8192, 2048], P('fsdp'), may hold values from -0.09375 to 0.09375
- down_weight: bfloat16 [64, 8192, 128], P('adapter', 'fsdp'), may hold values from -0.0625 to 0.0625
- up_projection_weight: bfloat16 [64, 64, 2048], P('adapter', None, 'fsdp'), may hold values from -0.75 to 0.75
- cotangent: bfloat16 [2048, 2048], P('adapter', 'fsdp'), may hold values from -3 to 3
Outputs:
- projected: bfloat16 [2048, 2048], P('adapter', 'fsdp')
- token_gradient: bfloat16 [2048, 8192], P('adapter', 'fsdp')
- down_weight_gradient: bfloat16 [64, 8192, 128], P('adapter', 'fsdp')
- up_weight_gradient: bfloat16 [64, 64, 2048], P('adapter', None, 'fsdp')
Inputs may be any that keep to these rules, and one draw needn't show every extreme that they name: `tenant`: adapter t belongs to owner t // 8. Among the 256 rows of one index of adapter at most 128 belong to the adapters of one owner, and one owner, the same for every index, has exactly 128 of them. send_list[i, o, :] lists in increasing order the rows (numbered within the 256 rows of index i of adapter) whose tenant belongs to owner o, then -1 in the slots left; every row stands in exactly one list.
All inputs are finite; a program needn't handle non-finite values.
Results may differ from a plain program's by a relative error of at most 0.005.
Values may be sent and summed in bfloat16 or wider, within the bound.
No kernel may reach another device: no remote copies, remote signals or barrier semaphores. Data moves between devices by JAX's collectives and lax.ppermute only.
A program may use at most 128 MiB of HBM per device.

v0:
```python
import jax
import jax.numpy as jnp
from jax import lax
from jax.sharding import PartitionSpec as P

KV = 1024
adapter_scale = 0.5


def down_partial(input_rows, weights_f, down_weight):
    low_all = jnp.einsum("sd,ldk->slk", input_rows, down_weight, preferred_element_type=jnp.float32)
    return jnp.sum(low_all * weights_f[:, :, None], axis=1)


def grad_partial(rows_dy, weights_f, up_projection_weight, selected_half):
    rank_size = up_projection_weight.shape[1]
    back_all = jnp.einsum(
        "sc,lrc->slr", rows_dy, up_projection_weight, preferred_element_type=jnp.float32
    )
    half_sum = jnp.sum(back_all * weights_f[:, :, None], axis=1)
    placed = jnp.zeros((rows_dy.shape[0], 2 * rank_size), jnp.float32)
    zero_idx = jnp.zeros((), jnp.int32)
    return lax.dynamic_update_slice(placed, half_sum, (zero_idx, selected_half * rank_size))


def forward_holder(low_rank, weight_table, up_projection_weight, selected_half):
    rank_size = up_projection_weight.shape[1]
    low_half = lax.dynamic_slice_in_dim(low_rank, selected_half * rank_size, rank_size, 1)
    broadcast_rows = low_half[:, None, :] * weight_table[:, :, None]
    adapter_update = adapter_scale * jnp.einsum(
        "slr,lrc->sc", broadcast_rows, up_projection_weight, preferred_element_type=jnp.float32
    )
    return (adapter_update.astype(jnp.bfloat16), broadcast_rows)


def backward_owner(back_low, weight_table, input_rows, rows_dy, broadcast_rows, down_weight):
    widened_rows = back_low[:, None, :] * weight_table[:, :, None]
    backward_update = adapter_scale * jnp.einsum(
        "wnr,nyr->wy", widened_rows, down_weight, preferred_element_type=jnp.float32
    )
    down_weight_gradient = adapter_scale * jnp.einsum(
        "wq,wmu->mqu", input_rows, widened_rows, preferred_element_type=jnp.float32
    )
    up_weight_gradient = adapter_scale * jnp.einsum(
        "slr,sc->lrc", broadcast_rows, rows_dy, preferred_element_type=jnp.float32
    )
    return (
        backward_update.astype(jnp.bfloat16),
        down_weight_gradient.astype(jnp.bfloat16),
        up_weight_gradient.astype(jnp.bfloat16),
    )


def shards(tokens, tenant, send_list, base_weight, down_weight, up_projection_weight, cotangent):
    rows_here = tokens.shape[0]
    width_here = tokens.shape[1]
    column_span = cotangent.shape[1]
    adapters_here = down_weight.shape[0]
    holder_list = send_list.shape[1]
    slot_capacity = send_list.shape[2]
    total_slots = holder_list * slot_capacity
    listed = send_list[0]
    present = listed >= 0
    safe_rows = jnp.where(present, listed, 0)
    local_ids = tenant % adapters_here
    picked_ids = local_ids[safe_rows]
    adapter_ids = jnp.arange(adapters_here, dtype=jnp.int32)
    selector = (
        (picked_ids[:, :, None] == adapter_ids[None, None, :]) & present[:, :, None]
    ).astype(jnp.bfloat16)
    send_x = tokens[safe_rows]
    send_dy = cotangent[safe_rows]
    drop_rows = jnp.where(present, listed, rows_here).reshape(total_slots)
    fsdp_pos = lax.axis_index("fsdp")
    selected_half = fsdp_pos * column_span // KV
    weight_cols = base_weight
    local_base_output = lax.psum_scatter(
        lax.dot_general(
            weight_cols, tokens, (((0,), (1,)), ((), ())), preferred_element_type=jnp.float32
        ),
        "fsdp",
        scatter_dimension=0,
        tiled=True,
    ).T
    weight_cols = base_weight
    input_frozen_part = lax.dot_general(
        lax.all_gather(cotangent, "fsdp", axis=1, tiled=True),
        weight_cols,
        (((1,), (1,)), ((), ())),
        preferred_element_type=jnp.float32,
    )
    recv_x, recv_sel = (
        lax.all_to_all(send_x, "adapter", split_axis=0, concat_axis=0, tiled=True),
        lax.all_to_all(selector, "adapter", split_axis=0, concat_axis=0, tiled=True),
    )
    input_rows = recv_x.reshape(total_slots, width_here)
    weight_table = recv_sel.reshape(total_slots, adapters_here)
    weights_f = weight_table.astype(jnp.float32)
    low_term = down_partial(input_rows, weights_f, down_weight)
    reduced_rank_sum = lax.psum(low_term, "fsdp")
    adapter_update, broadcast_rows = forward_holder(
        reduced_rank_sum.astype(jnp.bfloat16), weight_table, up_projection_weight, selected_half
    )
    got_delta = lax.all_to_all(
        adapter_update.reshape(holder_list, slot_capacity, column_span),
        "adapter",
        split_axis=0,
        concat_axis=0,
        tiled=True,
    )
    recv_dy = lax.all_to_all(send_dy, "adapter", split_axis=0, concat_axis=0, tiled=True)
    rows_dy = recv_dy.reshape(total_slots, column_span)
    back_sum = lax.psum(
        grad_partial(rows_dy, weights_f, up_projection_weight, selected_half), "fsdp"
    )
    backward_update, down_weight_gradient, up_weight_gradient = backward_owner(
        back_sum.astype(jnp.bfloat16),
        weight_table,
        input_rows,
        rows_dy,
        broadcast_rows,
        down_weight,
    )
    got_back = lax.all_to_all(
        backward_update.reshape(holder_list, slot_capacity, width_here),
        "adapter",
        split_axis=0,
        concat_axis=0,
        tiled=True,
    )
    adapter_columns = (
        jnp.zeros((rows_here, column_span), jnp.float32)
        .at[drop_rows]
        .add(got_delta.reshape(total_slots, column_span).astype(jnp.float32), mode="drop")
    )
    projected = (local_base_output + adapter_columns).astype(jnp.bfloat16)
    adapter_backward = (
        jnp.zeros((rows_here, width_here), jnp.float32)
        .at[drop_rows]
        .add(got_back.reshape(total_slots, width_here).astype(jnp.float32), mode="drop")
    )
    token_gradient = (input_frozen_part + adapter_backward).astype(jnp.bfloat16)
    return (projected, token_gradient, down_weight_gradient, up_weight_gradient)


def solution(mesh):
    in_specs = (
        P("adapter", "fsdp"),
        P("adapter"),
        P("adapter", None, None),
        P("fsdp", None),
        P("adapter", "fsdp", None),
        P("adapter", None, "fsdp"),
        P("adapter", "fsdp"),
    )
    out_specs = (
        P("adapter", "fsdp"),
        P("adapter", "fsdp"),
        P("adapter", "fsdp", None),
        P("adapter", None, "fsdp"),
    )
    return jax.shard_map(shards, mesh=mesh, in_specs=in_specs, out_specs=out_specs, check_vma=False)
```

profile of v0, /device:TPU:0, one launch (start us, length us, event | category | flops | bytes accessed | tf_op | source)
XLA Modules:
  0.0 267.3 jit_solution(12076343468223439721)
XLA Ops:
  9.4 6.8 %gather_fusion.1 = s32[1024]{0:T(1024)S(1)} fusion(s32[256]{0:T(256)S(1)} %and_select_fusion, s32[1024]{0:T(1024)S(1)} %fusion.29), kind=kCustom, calls=%fused_computation.1 | custom fusion | bytes 12288 | tf_op jit(solution)/shard_map/gather | solution.py:66
  16.8 5.2 %all-to-all-start.1 = ((bf16[8,128,8]{1,2,0:T(8,128)(2,1)}), bf16[8,128,8]{1,2,0:T(8,128)(2,1)S(1)}, u32[]{:S(2)}, u32[]{:S(2)}) async-start(bf16[8,128,8]{1,2,0:T(8,128)(2,1)} %fusion.27), calls=%async_computation.2 | async-start | bytes 32768 | tf_op jit(solution)/shard_map/all_to_all | solution.py:94
  22.0 5.1 %gather_fusion.2 = bf16[1024,512]{1,0:T(8,128)(2,1)} fusion(bf16[256,512]{1,0:T(8,128)(2,1)S(1)} %copy-done.1, s32[1024]{0:T(1024)S(1)} %fusion.29), kind=kCustom, calls=%fused_computation.2 | custom fusion | bytes 2101248 | tf_op jit(solution)/shard_map/gather | solution.py:72
  27.1 4.2 %all-to-all-start.3 = ((bf16[8,128,512]{2,1,0:T(8,128)(2,1)}), bf16[8,128,512]{2,1,0:T(8,128)(2,1)S(1)}, u32[]{:S(2)}, u32[]{:S(2)}) async-start(bf16[8,128,512]{2,1,0:T(8,128)(2,1)} %bitcast.14), calls=%async_computation.4 | async-start | bytes 2097152 | tf_op jit(solution)/shard_map/all_to_all | solution.py:111
  31.3 6.0 %gather_fusion = bf16[1024,2048]{1,0:T(8,128)(2,1)} fusion(bf16[256,2048]{1,0:T(8,128)(2,1)S(1)} %copy-done, s32[1024]{0:T(1024)S(1)} %fusion.29), kind=kCustom, calls=%fused_computation | custom fusion | bytes 8392704 | tf_op jit(solution)/shard_map/gather | solution.py:71
  37.2 9.4 %all-to-all-done.3 = bf16[8,128,512]{2,1,0:T(8,128)(2,1)S(1)} async-done(((bf16[8,128,512]{2,1,0:T(8,128)(2,1)}), bf16[8,128,512]{2,1,0:T(8,128)(2,1)S(1)}, u32[]{:S(2)}, u32[]{:S(2)}) %all-to-all-start.3) | async-done | bytes 1048608 | tf_op jit(solution)/shard_map/all_to_all | solution.py:111
  46.7 4.6 %all-to-all-start = ((bf16[8,128,2048]{2,1,0:T(8,128)(2,1)}), bf16[8,128,2048]{2,1,0:T(8,128)(2,1)}, u32[]{:S(2)}, u32[]{:S(2)}) async-start(bf16[8,128,2048]{2,1,0:T(8,128)(2,1)} %bitcast.50), calls=%async_computation.1 | async-start | bytes 8388608 | tf_op jit(solution)/shard_map/all_to_all | solution.py:93
  52.1 7.2 %fusion.31 = f32[2048,256]{1,0:T(8,128)} fusion(bf16[2048,2048]{1,0:T(8,128)(2,1)} %param.10, bf16[256,2048]{1,0:T(8,128)(2,1)S(1)} %copy-done), kind=kOutput, calls=%fused_computation.49 | convolution fusion | flops 2147483648 | bytes 11534336 | tf_op jit(solution)/shard_map/dot_general | solution.py:78
  60.2 40.2 %all-to-all-done = bf16[8,128,2048]{2,1,0:T(8,128)(2,1)} async-done(((bf16[8,128,2048]{2,1,0:T(8,128)(2,1)}), bf16[8,128,2048]{2,1,0:T(8,128)(2,1)}, u32[]{:S(2)}, u32[]{:S(2)}) %all-to-all-start) | async-done | bytes 4194336 | tf_op jit(solution)/shard_map/all_to_all | solution.py:93
  100.4 7.6 %multiply_reduce_fusion = f32[1024,128]{1,0:T(8,128)S(1)} fusion(bf16[1024,2048,1]{1,0,2:T(8,128)(2,1)} %bitcast.7, bf16[8,2048,128]{2,1,0:T(8,128)(2,1)} %param.11, f32[1024,8]{0,1:T(8,128)S(1)} %bitcast_convert_fusion), kind=kOutput, calls=%fused_computation.10 | convolution fusion | flops 4296933376 | bytes 8945664 | tf_op jit(solution)/shard_map/sd,ldk->slk/dot_general | solution.py:11
  107.9 56.5 %all-reduce.2 = (bf16[1024,128]{1,0:T(8,128)(2,1)S(1)}, bf16[1024,128]{0,1:T(8,128)(2,1)}) all-reduce(f32[1024,128]{1,0:T(8,128)S(1)} %multiply_reduce_fusion, f32[1024,128]{0,1:T(8,128)S(1)} %constant_dynamic-update-slice_fusion), channel_id=1, replica_groups=mesh['fsdp'=4,'adapter'=8] {'fsdp'}, use_global_device_ids=true, to_apply=%region_2.3 | all-reduce | flops 262144 | bytes 1572864 | tf_op jit(solution)/shard_map/psum | solution.py:100
  164.7 2.8 %fusion.8 = bf16[1024,512]{1,0:T(8,128)(2,1)} fusion(bf16[8,64,512]{2,1,0:T(8,128)(2,1)} %param.12, bf16[1024,8]{0,1:T(8,128)(2,1)S(1)} %bitcast.57, bf16[1024,64]{0,1:T(8,128)(2,1)S(1)} %copy.17), kind=kOutput, calls=%fused_computation.17 | convolution fusion | flops 538443776 | bytes 1720320 | tf_op jit(solution)/shard_map/slr,lrc->sc/dot_general | solution.py:30
  167.4 3.6 %all-to-all-start.2 = ((bf16[8,128,512]{2,1,0:T(8,128)(2,1)}), bf16[8,128,512]{2,1,0:T(8,128)(2,1)S(1)}, u32[]{:S(2)}, u32[]{:S(2)}) async-start(bf16[8,128,512]{2,1,0:T(8,128)(2,1)} %bitcast.55), calls=%async_computation.3 | async-start | bytes 2097152 | tf_op jit(solution)/shard_map/all_to_all | solution.py:104
  171.0 8.4 %fusion.2 = bf16[1024,2048]{1,0:T(8,128)(2,1)} fusion(bf16[8,2048,128]{2,1,0:T(8,128)(2,1)} %param.11, bf16[1024,8]{0,1:T(8,128)(2,1)S(1)} %bitcast.58, bf16[1024,128]{0,1:T(8,128)(2,1)} %get-tuple-element.17), kind=kOutput, calls=%fused_computation.8 | convolution fusion | flops 4300210176 | bytes 8667136 | tf_op jit(solution)/shard_map/wnr,nyr->wy/dot_general | solution.py:38
  179.4 7.0 %all-to-all-done.2 = bf16[8,128,512]{2,1,0:T(8,128)(2,1)S(1)} async-done(((bf16[8,128,512]{2,1,0:T(8,128)(2,1)}), bf16[8,128,512]{2,1,0:T(8,128)(2,1)S(1)}, u32[]{:S(2)}, u32[]{:S(2)}) %all-to-all-start.2) | async-done | bytes 1048608 | tf_op jit(solution)/shard_map/all_to_all | solution.py:104
  186.5 4.9 %all-to-all-start.4 = ((bf16[8,128,2048]{2,1,0:T(8,128)(2,1)}), bf16[8,128,2048]{2,1,0:T(8,128)(2,1)}, u32[]{:S(2)}, u32[]{:S(2)}) async-start(bf16[8,128,2048]{2,1,0:T(8,128)(2,1)} %bitcast.51), calls=%async_computation.5 | async-start | bytes 8388608 | tf_op jit(solution)/shard_map/all_to_all | solution.py:124
  191.4 7.4 %fusion.32 = f32[256,2048]{1,0:T(8,128)} fusion(bf16[256,2048]{1,0:T(8,128)(2,1)} %all-gather.2.cloned.1.call-done, bf16[2048,2048]{1,0:T(8,128)(2,1)} %param.10), kind=kOutput, calls=%fused_computation.50 | convolution fusion | flops 2147483648 | bytes 11534336 | tf_op jit(solution)/shard_map/dot_general | solution.py:86
  198.8 8.2 %fusion.3 = bf16[8,2048,128]{1,2,0:T(8,128)(2,1)} fusion(bf16[1024,2048,1]{1,0,2:T(8,128)(2,1)} %bitcast.7, bf16[1024,8]{0,1:T(8,128)(2,1)S(1)} %bitcast.59, bf16[1024,128]{0,1:T(8,128)(2,1)S(1)} %copy-done.4), kind=kOutput, calls=%fused_computation.11 | convolution fusion | flops 4300210176 | bytes 8667136 | tf_op jit(solution)/shard_map/wq,wmu->mqu/dot_general | solution.py:41
  207.1 6.4 %copy.20 = bf16[8,2048,128]{2,1,0:T(8,128)(2,1)} copy(bf16[8,2048,128]{1,2,0:T(8,128)(2,1)} %fusion.3) | data formatting | bytes 8388608
  213.5 1.5 fusion.15
  216.2 7.2 %scatter_custom_fusion = f32[256,512]{1,0:T(8,128)S(1)} fusion(f32[256,512]{1,0:T(8,128)S(1)} %copy.18, s32[1024]{0:T(1024)S(1)} %bitcast.63, bf16[1024,512]{1,0:T(8,128)(2,1)S(1)} %bitcast.52), kind=kCustom, calls=%fused_computation.14 | custom fusion | flops 1048576 | bytes 1572864 | tf_op jit(solution)/shard_map/scatter-add | solution.py:134
  224.1 16.1 %all-to-all-done.4 = bf16[8,128,2048]{2,1,0:T(8,128)(2,1)} async-done(((bf16[8,128,2048]{2,1,0:T(8,128)(2,1)}), bf16[8,128,2048]{2,1,0:T(8,128)(2,1)}, u32[]{:S(2)}, u32[]{:S(2)}) %all-to-all-start.4) | async-done | bytes 4194336 | tf_op jit(solution)/shard_map/all_to_all | solution.py:124
  240.3 17.5 %scatter_custom_fusion.1 = f32[256,2048]{1,0:T(8,128)} fusion(f32[256,2048]{1,0:T(8,128)} %fusion.32, s32[1024]{0:T(1024)S(1)} %bitcast.64, bf16[1024,2048]{1,0:T(8,128)(2,1)} %bitcast.24), kind=kCustom, calls=%fused_computation.5 | custom fusion | flops 4194304 | bytes 6291456 | tf_op jit(solution)/shard_map/scatter-add | solution.py:140
  257.8 2.7 %convert_element_type.60 = bf16[256,2048]{1,0:T(8,128)(2,1)} convert(f32[256,2048]{1,0:T(8,128)} %scatter_custom_fusion.1) | non-fusion elementwise | flops 524288 | bytes 3145728 | tf_op jit(solution)/shard_map/convert_element_type | solution.py:142
  (30 shorter events, 6.7 us)
Async XLA Ops:
  7.2 24.1 %copy-start = (bf16[256,2048]{1,0:T(8,128)(2,1)S(1)}, bf16[256,2048]{1,0:T(8,128)(2,1)}, u32[]{:S(2)}) copy-start(bf16[256,2048]{1,0:T(8,128)(2,1)} %param.7) | copy-start | bytes 3145732
  7.2 14.8 %copy-start.1 = (bf16[256,512]{1,0:T(8,128)(2,1)S(1)}, bf16[256,512]{1,0:T(8,128)(2,1)}, u32[]{:S(2)}) copy-start(bf16[256,512]{1,0:T(8,128)(2,1)} %param.13) | copy-start | bytes 786436
  16.8 10.3 %all-to-all-start.1 = ((bf16[8,128,8]{1,2,0:T(8,128)(2,1)}), bf16[8,128,8]{1,2,0:T(8,128)(2,1)S(1)}, u32[]{:S(2)}, u32[]{:S(2)}) async-start(bf16[8,128,8]{1,2,0:T(8,128)(2,1)} %fusion.27), calls=%async_computation.2 | async-start | bytes 32768 | tf_op jit(solution)/shard_map/all_to_all | solution.py:94
  27.1 19.6 %all-to-all-start.3 = ((bf16[8,128,512]{2,1,0:T(8,128)(2,1)}), bf16[8,128,512]{2,1,0:T(8,128)(2,1)S(1)}, u32[]{:S(2)}, u32[]{:S(2)}) async-start(bf16[8,128,512]{2,1,0:T(8,128)(2,1)} %bitcast.14), calls=%async_computation.4 | async-start | bytes 2097152 | tf_op jit(solution)/shard_map/all_to_all | solution.py:111
  46.7 53.7 %all-to-all-start = ((bf16[8,128,2048]{2,1,0:T(8,128)(2,1)}), bf16[8,128,2048]{2,1,0:T(8,128)(2,1)}, u32[]{:S(2)}, u32[]{:S(2)}) async-start(bf16[8,128,2048]{2,1,0:T(8,128)(2,1)} %bitcast.50), calls=%async_computation.1 | async-start | bytes 8388608 | tf_op jit(solution)/shard_map/all_to_all | solution.py:93
  51.3 140.1 %all-gather.2.cloned.1.call-start = ((), (), s32[]{:S(2)}) async-start(), calls=%async_computation.7 | async-start | bytes 1310720 | tf_op jit(solution)/shard_map/all_gather | solution.py:87
  52.0 7.3 %copy-start.3 = (bf16[8,64,512]{2,1,0:T(8,128)(2,1)S(1)}, bf16[8,64,512]{2,1,0:T(8,128)(2,1)}, u32[]{:S(2)}) copy-start(bf16[8,64,512]{2,1,0:T(8,128)(2,1)} %param.12) | copy-start | bytes 1572868
  52.0 163.0 %reduce-scatter.2.cloned.1.call-start = ((), (), s32[]{:S(2)}) async-start(), calls=%async_computation.6 | async-start | bytes 2621440 | tf_op jit(solution)/shard_map/reduce_scatter | solution.py:77
  167.4 19.0 %all-to-all-start.2 = ((bf16[8,128,512]{2,1,0:T(8,128)(2,1)}), bf16[8,128,512]{2,1,0:T(8,128)(2,1)S(1)}, u32[]{:S(2)}, u32[]{:S(2)}) async-start(bf16[8,128,512]{2,1,0:T(8,128)(2,1)} %bitcast.55), calls=%async_computation.3 | async-start | bytes 2097152 | tf_op jit(solution)/shard_map/all_to_all | solution.py:104
  186.5 4.9 %copy-start.2 = (s32[1,8,128]{2,1,0:T(8,128)S(1)}, s32[1,8,128]{2,1,0:T(8,128)}, u32[]{:S(2)}) copy-start(s32[1,8,128]{2,1,0:T(8,128)} %param.9) | copy-start | bytes 12292
  186.5 53.8 %all-to-all-start.4 = ((bf16[8,128,2048]{2,1,0:T(8,128)(2,1)}), bf16[8,128,2048]{2,1,0:T(8,128)(2,1)}, u32[]{:S(2)}, u32[]{:S(2)}) async-start(bf16[8,128,2048]{2,1,0:T(8,128)(2,1)} %bitcast.51), calls=%async_computation.5 | async-start | bytes 8388608 | tf_op jit(solution)/shard_map/all_to_all | solution.py:124
  191.4 7.5 %copy-start.4 = (bf16[1024,128]{0,1:T(8,128)(2,1)S(1)}, bf16[1024,128]{0,1:T(8,128)(2,1)}, u32[]{:S(2)}) copy-start(bf16[1024,128]{0,1:T(8,128)(2,1)} %get-tuple-element.17) | copy-start | bytes 786436
Sparse Core Ops, SparseCore 0:
  53.7 29.5 all-gather.1
  85.5 58.0 reduce-scatter.1
where the time goes:
time: 268 us; the launch traced here: 267 us
  waiting for transfers between devices  73.5 us (27%)
  blocking collectives  56.5 us (21%)
  matrix products  43.9 us (16%)
  other arithmetic  30.9 us (12%)
  local copies, waits for them, and re-layouts  25.9 us (10%)
  starting transfers between devices  22.5 us (8%)
  between operations  14.2 us (5%)
    psum x1, blocking collectives, shards(): reduced_rank_sum = lax.psum(low_term, 'fsdp')  56.5 us
    all_to_all x1, waiting for transfers between devices, shards(): lax.all_to_all(send_x, 'adapter', split_axis=0, concat_axis=0, tiled=True)  40.2 us
    scatter-add x1, other arithmetic, shards(): adapter_backward = jnp.zeros((rows_here, width_here), jnp.float32).at[dro...  17.5 us
    all_to_all x1, waiting for transfers between devices, shards(): lax.all_to_all(backward_update.reshape(holder_list, slot_capacity, width_...  16.1 us
    all_to_all x1, waiting for transfers between devices, shards(): lax.all_to_all(send_dy, 'adapter', split_axis=0, concat_axis=0, tiled=True)  9.44 us
    dot_general x1, matrix products, backward_owner(): jnp.einsum('wnr,nyr->wy', widened_rows, down_weight, preferred_element_ty...  8.41 us
    dot_general x1, matrix products, backward_owner(): jnp.einsum('wq,wmu->mqu', input_rows, widened_rows, preferred_element_typ...  8.22 us
    dot_general x1, matrix products, down_partial(): jnp.einsum('sd,ldk->slk', input_rows, down_weight, preferred_element_type...  7.56 us
  transfers between devices with their start and end apart: 7, of which 4 were waited for; matrix products, arithmetic and copies ran while one was open for 26% of the time, Pallas kernels for 0%

commit v1 on v0

--- a/solution.py
+++ b/solution.py
@@ -97,7 +97,11 @@
     weight_table = recv_sel.reshape(total_slots, adapters_here)
     weights_f = weight_table.astype(jnp.float32)
     low_term = down_partial(input_rows, weights_f, down_weight)
-    reduced_rank_sum = lax.psum(low_term, "fsdp")
+    reduced_rank_sum = low_term
+    for hop in (1, 2):
+        reduced_rank_sum = reduced_rank_sum + lax.ppermute(
+            reduced_rank_sum, "fsdp", [(dev, dev ^ hop) for dev in range(4)]
+        )
     adapter_update, broadcast_rows = forward_holder(
         reduced_rank_sum.astype(jnp.bfloat16), weight_table, up_projection_weight, selected_half
     )

time: 268 us -> 248 us (0.925)
  blocking collectives: 56.5 us -> 40.8 us
  waiting for transfers between devices: 73.5 us -> 68.8 us
    ppermute x0 -> x2, waiting for transfers between devices: none -> 58.6 us  [shards(): lax.ppermute(reduced_rank_sum, 'fsdp', [(dev, dev ^ hop) for dev in range...]
    all_to_all x1, waiting for transfers between devices: 40.2 us -> 0.01 us  [shards(): lax.all_to_all(send_x, 'adapter', split_axis=0, concat_axis=0, tiled=True)]
    all_to_all x1, waiting for transfers between devices: 16.1 us -> 0.01 us  [shards(): lax.all_to_all(backward_update.reshape(holder_list, slot_capacity, width_...]
    psum x1, blocking collectives: 56.5 us -> 40.8 us  [shards(): lax.psum(grad_partial(rows_dy, weights_f, up_projection_weight, selected_...]
    all_to_all x1, waiting for transfers between devices: 7 us -> 0.01 us  [shards(): lax.all_to_all(adapter_update.reshape(holder_list, slot_capacity, column_...]
  transfers between devices with their start and end apart: 7 -> 9, of which waited for: 4 -> 3; matrix products, arithmetic and copies ran while one was open for 26% -> 34% of each run, Pallas kernels for 0% -> 0%
where the time goes in v1:
time: 248 us
  waiting for transfers between devices  68.8 us (28%)
  matrix products  44.1 us (18%)
  blocking collectives  40.8 us (16%)
  other arithmetic  31.1 us (13%)
  local copies, waits for them, and re-layouts  25.8 us (10%)
  starting transfers between devices  22.8 us (9%)
  between operations  14.3 us (6%)
    ppermute x2, waiting for transfers between devices, shards(): lax.ppermute(reduced_rank_sum, 'fsdp', [(dev, dev ^ hop) for dev in range...  58.6 us
    psum x1, blocking collectives, shards(): lax.psum(grad_partial(rows_dy, weights_f, up_projection_weight, selected_...  40.8 us
    scatter-add x1, other arithmetic, shards(): adapter_backward = jnp.zeros((rows_here, width_here), jnp.float32).at[dro...  17.5 us
    all_to_all x1, waiting for transfers between devices, shards(): lax.all_to_all(send_dy, 'adapter', split_axis=0, concat_axis=0, tiled=True)  9.44 us
    dot_general x1, matrix products, backward_owner(): jnp.einsum('wnr,nyr->wy', widened_rows, down_weight, preferred_element_ty...  8.35 us
    dot_general x1, matrix products, backward_owner(): jnp.einsum('wq,wmu->mqu', input_rows, widened_rows, preferred_element_typ...  8.23 us
    dot_general x1, matrix products, down_partial(): jnp.einsum('sd,ldk->slk', input_rows, down_weight, preferred_element_type...  7.58 us
    dot_general x1, matrix products, shards(): lax.dot_general(lax.all_gather(cotangent, 'fsdp', axis=1, tiled=True), we...  7.46 us
  transfers between devices with their start and end apart: 9, of which 3 were waited for; matrix products, arithmetic and copies ran while one was open for 34% of the time, Pallas kernels for 0%

profile of v1, /device:TPU:0, one launch (start us, length us, event | category | flops | bytes accessed | tf_op | source)
XLA Modules:
  0.0 247.6 jit_solution(2950720111783867780)
XLA Ops:
  9.4 6.8 %gather_fusion.1 = s32[1024]{0:T(1024)S(1)} fusion(s32[256]{0:T(256)S(1)} %and_select_fusion, s32[1024]{0:T(1024)S(1)} %fusion.30), kind=kCustom, calls=%fused_computation.1 | custom fusion | bytes 12288 | tf_op jit(solution)/shard_map/gather | solution.py:66
  16.8 5.2 %all-to-all-start.1 = ((bf16[8,128,8]{1,2,0:T(8,128)(2,1)}), bf16[8,128,8]{1,2,0:T(8,128)(2,1)S(1)}, u32[]{:S(2)}, u32[]{:S(2)}) async-start(bf16[8,128,8]{1,2,0:T(8,128)(2,1)} %fusion.28), calls=%async_computation.2 | async-start | bytes 32768 | tf_op jit(solution)/shard_map/all_to_all | solution.py:94
  22.0 5.1 %gather_fusion.2 = bf16[1024,512]{1,0:T(8,128)(2,1)} fusion(bf16[256,512]{1,0:T(8,128)(2,1)S(1)} %copy-done.1, s32[1024]{0:T(1024)S(1)} %fusion.30), kind=kCustom, calls=%fused_computation.2 | custom fusion | bytes 2101248 | tf_op jit(solution)/shard_map/gather | solution.py:72
  27.1 4.2 %all-to-all-start.3 = ((bf16[8,128,512]{2,1,0:T(8,128)(2,1)}), bf16[8,128,512]{2,1,0:T(8,128)(2,1)S(1)}, u32[]{:S(2)}, u32[]{:S(2)}) async-start(bf16[8,128,512]{2,1,0:T(8,128)(2,1)} %bitcast.14), calls=%async_computation.4 | async-start | bytes 2097152 | tf_op jit(solution)/shard_map/all_to_all | solution.py:115
  31.3 6.0 %gather_fusion = bf16[1024,2048]{1,0:T(8,128)(2,1)} fusion(bf16[256,2048]{1,0:T(8,128)(2,1)S(1)} %copy-done, s32[1024]{0:T(1024)S(1)} %fusion.30), kind=kCustom, calls=%fused_computation | custom fusion | bytes 8392704 | tf_op jit(solution)/shard_map/gather | solution.py:71
  37.2 9.4 %all-to-all-done.3 = bf16[8,128,512]{2,1,0:T(8,128)(2,1)S(1)} async-done(((bf16[8,128,512]{2,1,0:T(8,128)(2,1)}), bf16[8,128,512]{2,1,0:T(8,128)(2,1)S(1)}, u32[]{:S(2)}, u32[]{:S(2)}) %all-to-all-start.3) | async-done | bytes 1048608 | tf_op jit(solution)/shard_map/all_to_all | solution.py:115
  46.7 4.7 %all-to-all-start = ((bf16[8,128,2048]{2,1,0:T(8,128)(2,1)}), bf16[8,128,2048]{2,1,0:T(8,128)(2,1)}, u32[]{:S(2)}, u32[]{:S(2)}) async-start(bf16[8,128,2048]{2,1,0:T(8,128)(2,1)} %bitcast.50), calls=%async_computation.1 | async-start | bytes 8388608 | tf_op jit(solution)/shard_map/all_to_all | solution.py:93
  53.0 40.8 %all-reduce.1 = bf16[1024,128]{0,1:T(8,128)(2,1)S(1)} all-reduce(f32[1024,128]{0,1:T(8,128)S(1)} %constant_dynamic-update-slice_fusion), channel_id=1, replica_groups=mesh['fsdp'=4,'adapter'=8] {'fsdp'}, use_global_device_ids=true, to_apply=%region_4.5 | all-reduce | flops 131072 | bytes 786432 | tf_op jit(solution)/shard_map/psum | solution.py:117
  93.9 8.3 %fusion.2 = bf16[1024,2048]{1,0:T(8,128)(2,1)} fusion(bf16[8,2048,128]{2,1,0:T(8,128)(2,1)} %param.11, bf16[1024,8]{0,1:T(8,128)(2,1)S(1)} %bitcast.56, bf16[1024,128]{0,1:T(8,128)(2,1)S(1)} %all-reduce.1), kind=kOutput, calls=%fused_computation.8 | convolution fusion | flops 4300210176 | bytes 8667136 | tf_op jit(solution)/shard_map/wnr,nyr->wy/dot_general | solution.py:38
  102.2 4.5 %all-to-all-start.4 = ((bf16[8,128,2048]{2,1,0:T(8,128)(2,1)}), bf16[8,128,2048]{2,1,0:T(8,128)(2,1)}, u32[]{:S(2)}, u32[]{:S(2)}) async-start(bf16[8,128,2048]{2,1,0:T(8,128)(2,1)} %bitcast.51), calls=%async_computation.5 | async-start | bytes 8388608 | tf_op jit(solution)/shard_map/all_to_all | solution.py:128
  107.0 7.2 %fusion.32 = f32[2048,256]{1,0:T(8,128)} fusion(bf16[2048,2048]{1,0:T(8,128)(2,1)} %param.10, bf16[256,2048]{1,0:T(8,128)(2,1)S(1)} %copy-done), kind=kOutput, calls=%fused_computation.50 | convolution fusion | flops 2147483648 | bytes 11534336 | tf_op jit(solution)/shard_map/dot_general | solution.py:78
  114.2 7.6 %multiply_reduce_fusion = f32[1024,128]{1,0:T(8,128)S(1)} fusion(bf16[1024,2048,1]{1,0,2:T(8,128)(2,1)} %bitcast.7, bf16[8,2048,128]{2,1,0:T(8,128)(2,1)} %param.11, f32[1024,8]{0,1:T(8,128)S(1)} %bitcast_convert_fusion), kind=kOutput, calls=%fused_computation.10 | convolution fusion | flops 4296933376 | bytes 8945664 | tf_op jit(solution)/shard_map/sd,ldk->slk/dot_general | solution.py:11
  121.9 36.5 %collective-permute-done = f32[1024,128]{1,0:T(8,128)S(1)} collective-permute-done((f32[1024,128]{1,0:T(8,128)S(1)}, f32[1024,128]{1,0:T(8,128)S(1)}, u32[]{:S(2)}, u32[]{:S(2)}) %collective-permute-start) | collective-permute-done | bytes 524320 | tf_op jit(solution)/shard_map/ppermute | solution.py:102
  158.6 7.5 %fusion.33 = f32[256,2048]{1,0:T(8,128)} fusion(bf16[256,2048]{1,0:T(8,128)(2,1)} %all-gather.2.cloned.1.call-done, bf16[2048,2048]{1,0:T(8,128)(2,1)} %param.10), kind=kOutput, calls=%fused_computation.51 | convolution fusion | flops 2147483648 | bytes 11534336 | tf_op jit(solution)/shard_map/dot_general | solution.py:86
  166.0 22.1 %collective-permute-done.1 = f32[1024,128]{1,0:T(8,128)S(1)} collective-permute-done((f32[1024,128]{1,0:T(8,128)S(1)}, f32[1024,128]{1,0:T(8,128)S(1)}, u32[]{:S(2)}, u32[]{:S(2)}) %collective-permute-start.1) | collective-permute-done | bytes 524320 | tf_op jit(solution)/shard_map/ppermute | solution.py:102
  188.6 1.8 fusion.8
  190.4 3.8 %all-to-all-start.2 = ((bf16[8,128,512]{2,1,0:T(8,128)(2,1)}), bf16[8,128,512]{2,1,0:T(8,128)(2,1)S(1)}, u32[]{:S(2)}, u32[]{:S(2)}) async-start(bf16[8,128,512]{2,1,0:T(8,128)(2,1)} %bitcast.12), calls=%async_computation.3 | async-start | bytes 2097152 | tf_op jit(solution)/shard_map/all_to_all | solution.py:108
  194.2 8.2 %fusion.3 = bf16[8,2048,128]{1,2,0:T(8,128)(2,1)} fusion(bf16[1024,2048,1]{1,0,2:T(8,128)(2,1)} %bitcast.7, bf16[1024,8]{0,1:T(8,128)(2,1)S(1)} %bitcast.58, bf16[1024,128]{0,1:T(8,128)(2,1)S(1)} %all-reduce.1), kind=kOutput, calls=%fused_computation.11 | convolution fusion | flops 4300210176 | bytes 8667136 | tf_op jit(solution)/shard_map/wq,wmu->mqu/dot_general | solution.py:41
  202.4 6.4 %copy.20 = bf16[8,2048,128]{2,1,0:T(8,128)(2,1)} copy(bf16[8,2048,128]{1,2,0:T(8,128)(2,1)} %fusion.3) | data formatting | bytes 8388608
  208.8 1.2 copy.18
  210.1 17.5 %scatter_custom_fusion.1 = f32[256,2048]{1,0:T(8,128)} fusion(f32[256,2048]{1,0:T(8,128)} %fusion.33, s32[1024]{0:T(1024)S(1)} %bitcast.62, bf16[1024,2048]{1,0:T(8,128)(2,1)} %bitcast.24), kind=kCustom, calls=%fused_computation.5 | custom fusion | flops 4194304 | bytes 6291456 | tf_op jit(solution)/shard_map/scatter-add | solution.py:144
  227.6 2.7 %convert_element_type.60 = bf16[256,2048]{1,0:T(8,128)(2,1)} convert(f32[256,2048]{1,0:T(8,128)} %scatter_custom_fusion.1) | non-fusion elementwise | flops 524288 | bytes 3145728 | tf_op jit(solution)/shard_map/convert_element_type | solution.py:146
  230.3 2.7 %fusion.15 = bf16[8,64,512]{2,1,0:T(8,128)(2,1)} fusion(bf16[1024,512,1]{1,0,2:T(8,128)(2,1)} %bitcast.54, bf16[1024,8]{0,1:T(8,128)(2,1)S(1)} %bitcast.59, bf16[1024,64]{0,1:T(8,128)(2,1)S(1)} %copy.17), kind=kOutput, calls=%fused_computation.23 | convolution fusion | flops 537919488 | bytes 1720320 | tf_op jit(solution)/shard_map/slr,sc->lrc/dot_general | solution.py:44
  233.0 6.9 %scatter_custom_fusion = f32[256,512]{1,0:T(8,128)S(1)} fusion(f32[256,512]{1,0:T(8,128)S(1)} %copy.18, s32[1024]{0:T(1024)S(1)} %bitcast.63, bf16[1024,512]{1,0:T(8,128)(2,1)S(1)} %bitcast.52), kind=kCustom, calls=%fused_computation.14 | custom fusion | flops 1048576 | bytes 1572864 | tf_op jit(solution)/shard_map/scatter-add | solution.py:138
  (35 shorter events, 6.0 us)
Async XLA Ops:
  7.2 24.1 %copy-start = (bf16[256,2048]{1,0:T(8,128)(2,1)S(1)}, bf16[256,2048]{1,0:T(8,128)(2,1)}, u32[]{:S(2)}) copy-start(bf16[256,2048]{1,0:T(8,128)(2,1)} %param.7) | copy-start | bytes 3145732
  7.2 14.8 %copy-start.1 = (bf16[256,512]{1,0:T(8,128)(2,1)S(1)}, bf16[256,512]{1,0:T(8,128)(2,1)}, u32[]{:S(2)}) copy-start(bf16[256,512]{1,0:T(8,128)(2,1)} %param.13) | copy-start | bytes 786436
  16.8 10.3 %all-to-all-start.1 = ((bf16[8,128,8]{1,2,0:T(8,128)(2,1)}), bf16[8,128,8]{1,2,0:T(8,128)(2,1)S(1)}, u32[]{:S(2)}, u32[]{:S(2)}) async-start(bf16[8,128,8]{1,2,0:T(8,128)(2,1)} %fusion.28), calls=%async_computation.2 | async-start | bytes 32768 | tf_op jit(solution)/shard_map/all_to_all | solution.py:94
  27.1 19.6 %all-to-all-start.3 = ((bf16[8,128,512]{2,1,0:T(8,128)(2,1)}), bf16[8,128,512]{2,1,0:T(8,128)(2,1)S(1)}, u32[]{:S(2)}, u32[]{:S(2)}) async-start(bf16[8,128,512]{2,1,0:T(8,128)(2,1)} %bitcast.14), calls=%async_computation.4 | async-start | bytes 2097152 | tf_op jit(solution)/shard_map/all_to_all | solution.py:115
  46.7 5.5 %copy-start.2 = (bf16[8,128,512]{2,1,0:T(8,128)(2,1)}, bf16[8,128,512]{2,1,0:T(8,128)(2,1)S(1)}, u32[]{:S(2)}) copy-start(bf16[8,128,512]{2,1,0:T(8,128)(2,1)S(1)} %all-to-all-done.3) | copy-start | bytes 3145732
  46.7 5.5 %copy-start.4 = (bf16[8,64,512]{2,1,0:T(8,128)(2,1)S(1)}, bf16[8,64,512]{2,1,0:T(8,128)(2,1)}, u32[]{:S(2)}) copy-start(bf16[8,64,512]{2,1,0:T(8,128)(2,1)} %param.12) | copy-start | bytes 1572868
  46.7 55.5 %all-to-all-start = ((bf16[8,128,2048]{2,1,0:T(8,128)(2,1)}), bf16[8,128,2048]{2,1,0:T(8,128)(2,1)}, u32[]{:S(2)}, u32[]{:S(2)}) async-start(bf16[8,128,2048]{2,1,0:T(8,128)(2,1)} %bitcast.50), calls=%async_computation.1 | async-start | bytes 8388608 | tf_op jit(solution)/shard_map/all_to_all | solution.py:93
  51.4 107.2 %all-gather.2.cloned.1.call-start = ((), (), s32[]{:S(2)}) async-start(), calls=%async_computation.7 | async-start | bytes 1310720 | tf_op jit(solution)/shard_map/all_gather | solution.py:87
  102.2 88.2 %all-to-all-start.4 = ((bf16[8,128,2048]{2,1,0:T(8,128)(2,1)}), bf16[8,128,2048]{2,1,0:T(8,128)(2,1)}, u32[]{:S(2)}, u32[]{:S(2)}) async-start(bf16[8,128,2048]{2,1,0:T(8,128)(2,1)} %bitcast.51), calls=%async_computation.5 | async-start | bytes 8388608 | tf_op jit(solution)/shard_map/all_to_all | solution.py:128
  106.8 102.1 %reduce-scatter.2.cloned.1.call-start = ((), (), s32[]{:S(2)}) async-start(), calls=%async_computation.6 | async-start | bytes 2621440 | tf_op jit(solution)/shard_map/reduce_scatter | solution.py:77
  114.2 7.7 %copy-start.3 = (s32[1,8,128]{2,1,0:T(8,128)S(1)}, s32[1,8,128]{2,1,0:T(8,128)}, u32[]{:S(2)}) copy-start(s32[1,8,128]{2,1,0:T(8,128)} %param.9) | copy-start | bytes 12292
  121.8 36.6 %collective-permute-start = (f32[1024,128]{1,0:T(8,128)S(1)}, f32[1024,128]{1,0:T(8,128)S(1)}, u32[]{:S(2)}, u32[]{:S(2)}) collective-permute-start(f32[1024,128]{1,0:T(8,128)S(1)} %multiply_reduce_fusion), channel_id=1, source_target_pairs={{0,8},{8,0},{16,24},{24,16},{1,9},{9,1},{17,25},{25,17},{2,10},{10... | collective-permute-start | bytes 1572872 | tf_op jit(solution)/shard_map/ppermute | solution.py:102
  158.5 29.7 %collective-permute-start.1 = (f32[1024,128]{1,0:T(8,128)S(1)}, f32[1024,128]{1,0:T(8,128)S(1)}, u32[]{:S(2)}, u32[]{:S(2)}) collective-permute-start(f32[1024,128]{1,0:T(8,128)S(1)} %add.55), channel_id=1, source_target_pairs={{0,16},{8,24},{16,0},{24,8},{1,17},{9,25},{17,1},{25,9},{2,18},{10... | collective-permute-start | bytes 1572872 | tf_op jit(solution)/shard_map/ppermute | solution.py:102
  190.4 42.6 %all-to-all-start.2 = ((bf16[8,128,512]{2,1,0:T(8,128)(2,1)}), bf16[8,128,512]{2,1,0:T(8,128)(2,1)S(1)}, u32[]{:S(2)}, u32[]{:S(2)}) async-start(bf16[8,128,512]{2,1,0:T(8,128)(2,1)} %bitcast.12), calls=%async_computation.3 | async-start | bytes 2097152 | tf_op jit(solution)/shard_map/all_to_all | solution.py:108
Sparse Core Ops, SparseCore 0:
  53.8 40.9 all-gather.1
  114.3 62.0 reduce-scatter.1
